TPU v7x, 256 devices: a whole 4x4x8 slice. The times are simulated.
256 devices in a mesh: lon: 8 (over y, x_lo), lat: 16 (over z, x_hi), rep: 2 (over core).
Axes of the slice: x: 4 (x_hi: 2, x_lo: 2; x = x_hi * 2 + x_lo), y: 4, z: 8, core: 2. Of those that a mesh axis runs over, the one named last changes fastest.
Arguments:
- forcing: float32 [8, 4, 2, 512, 2048], P('rep', None, None, 'lat', 'lon'), may hold values from -6 to 6
- diffusivity: float32 [512, 2048], P('lat', 'lon'), may hold values from 0.1 to 0.22
- ocean: int32 [512, 2048], P('lat', 'lon'), may hold values 0 or 1
- phase: float32 [4], replicated, may hold values from 0.1 to 0.4
- site_cell: int32 [16, 8, 2048], P('lat', 'lon'), may hold values from 0 to 8191
- site_count: int32 [16, 8], P('lat', 'lon'), may hold values from 1 to 2048, 10240 in all within a row
- site_weight: float32 [16, 8, 2048], P('lat', 'lon'), may hold values from 0.5 to 5
Outputs:
- representer: float32 [8, 4, 2, 512, 2048], P('rep', None, None, 'lat', 'lon')
- gram: float32 [8, 8], P('rep')
Inputs may be any that keep to these rules, and one draw needn't show every extreme that they name: `site_count`: live slots are the first ones of a block; in each latitude row of blocks one block has all 2048 slots live.
All inputs are finite; a program needn't handle non-finite values. No bound on the sum of `ocean` on one device may be relied on, other than what follows from the above.
Results may differ from a plain program's by a relative error of at most 0.00007.
Values sent between devices are 32-bit elements; how exact they have to be, the bound alone decides.
A program may use at most 64 MiB of HBM per device.

v0:
```python
import jax
import jax.numpy as jnp
from jax import lax
from jax.sharding import Mesh
from jax.sharding import PartitionSpec as P

CONST = 4
SWEEPS = 4
LAT = ("lat_0", "lat_1")
LON_LAT = ("lon_0", "lon_1", "lat_0", "lat_1")
LON = ("lon_0", "lon_1")
DAMPING = 0.9


def padded_2(shard, sides, width):
    for axis, dim in sides:
        devices, length = (lax.axis_size(axis), shard.shape[dim])
        up = [(i, (i + 1) % devices) for i in range(devices)]
        down = [(j, i) for i, j in up]
        last = lax.slice_in_dim(shard, length - width, length, axis=dim)
        leading = lax.slice_in_dim(shard, 0, width, axis=dim)
        before = lax.ppermute(last, axis, up)
        after = lax.ppermute(leading, axis, down)
        shard = jnp.concatenate([before, shard, after], axis=dim)
    return shard


def copy_for_each(shard, axis):
    copies = jnp.broadcast_to(shard, (lax.axis_size(axis), *shard.shape))
    return lax.all_to_all(copies, axis, split_axis=0, concat_axis=0, tiled=True)


def laid_out(pieces, dim):
    pieces = jnp.moveaxis(pieces, 0, dim)
    dims = pieces.shape
    return pieces.reshape(*dims[:dim], dims[dim] * dims[dim + 1], *dims[dim + 2 :])


def gather_directly(shard, axis, dim):
    pieces = copy_for_each(shard, axis)
    return laid_out(pieces, dim)


def one_axis_at_a_time(shard, axes):
    for axis in axes:
        shard = lax.psum(shard, axis)
    return shard


def laplace(padded):
    center = padded[..., 1:-1, 1:-1]
    total = (
        padded[..., 2:, 1:-1]
        + padded[..., :-2, 1:-1]
        + padded[..., 1:-1, 2:]
        + padded[..., 1:-1, :-2]
    )
    return total - 4.0 * center


def rotate(field, cosine, sinus):
    real_part = field[:, :, 0]
    imag_part = field[:, :, 1]
    new_real = cosine * real_part - sinus * imag_part
    new_imag = sinus * real_part + cosine * imag_part
    return jnp.stack([new_real, new_imag], axis=2)


def lat_valid(rows_lat, width):
    first = lax.axis_index(LAT) * rows_lat - width
    latitude = first + jnp.arange(rows_lat + 2 * width, dtype=jnp.int32)
    inside = (latitude >= 0) & (latitude < rows_lat * lax.axis_size(LAT))
    return inside.astype(jnp.float32)[:, None]


def local(forcing, diffusivity, ocean, phase, site_cell, site_count, site_weight):
    rows_lat = forcing.shape[3]
    cols_lon = forcing.shape[4]
    wet = ocean.astype(jnp.float32)
    cosine = jnp.cos(phase)[:, None, None]
    sinus = jnp.sin(phase)[:, None, None]
    depth = SWEEPS
    deep_valid = lat_valid(rows_lat, depth)
    coefficients = jnp.stack([diffusivity, wet], axis=0)
    extended = padded_2(coefficients, ((LON, 2), (LAT, 1)), depth) * deep_valid
    diffuse_ext = extended[0]
    wet_ext = extended[1]

    def window(array, width):
        start = depth - width
        return array[start : start + rows_lat + 2 * width, start : start + cols_lon + 2 * width]

    current = padded_2(forcing, ((LON, 4), (LAT, 3)), depth) * deep_valid
    for step in range(SWEEPS):
        width = depth - step
        product = window(diffuse_ext, width) * current
        inner = current[..., 1:-1, 1:-1]
        current = window(wet_ext, width - 1) * (
            DAMPING * rotate(inner, cosine, -sinus) + laplace(product)
        )
    current = padded_2(current, ((LON, 4), (LAT, 3)), depth) * deep_valid
    for step in range(SWEEPS):
        width = depth - step
        inner = current[..., 1:-1, 1:-1]
        current = window(wet_ext, width - 1) * (
            DAMPING * rotate(inner, cosine, sinus)
            + window(diffuse_ext, width - 1) * laplace(current)
        )
    rep_local = current.shape[0]
    slot_total = site_cell.shape[2]
    flat = current.reshape(rep_local, CONST * 2, rows_lat * cols_lon)
    samples = jnp.take(flat, site_cell[0, 0], axis=2)
    slots = jnp.arange(slot_total, dtype=jnp.int32)
    weight = site_weight[0, 0] * (slots < site_count[0, 0]).astype(jnp.float32)
    weighted = (samples * weight[None, None, :]).reshape(rep_local, -1)
    plain = samples.reshape(rep_local, -1)
    gathered = gather_directly(plain, "rep", 0)
    partial_rows = jnp.dot(
        weighted, gathered.T, precision=lax.Precision.HIGHEST, preferred_element_type=jnp.float32
    )
    scale = float(lax.axis_size(LAT) * lax.axis_size(LON) * slot_total)
    gram = one_axis_at_a_time(partial_rows, LON_LAT) / scale
    return (current, gram)


def solution(mesh):
    torus = Mesh(
        mesh.devices.reshape(4, 2, 8, 2, mesh.shape["rep"]),
        ("lon_0", "lon_1", "lat_0", "lat_1", "rep"),
    )
    return jax.shard_map(
        local,
        mesh=torus,
        in_specs=(
            P("rep", None, None, LAT, LON),
            P(LAT, LON),
            P(LAT, LON),
            P(),
            P(LAT, LON, None),
            P(LAT, LON),
            P(LAT, LON, None),
        ),
        out_specs=(P("rep", None, None, LAT, LON), P("rep", None)),
        check_vma=False,
    )
```

profile of v0, /device:TPU:2, one launch (start us, length us, event | category | flops | bytes accessed | tf_op | source)
XLA Modules:
  0.0 189.4 jit_solution(609035854693240836)
XLA Ops:
  6.1 2.2 %collective-permute-start.4 = (f32[4,4,2,32,4]{4,3,2,1,0:T(8,128)S(1)}, f32[4,4,2,32,4]{4,3,2,1,0:T(8,128)S(1)}, u32[]{:S(2)}, u32[]{:S(2)}) collective-permute-start(f32[4,4,2,32,4]{4,3,2,1,0:T(8,128)S(1)} %get-tuple-element.32), channel_id=1, source_target_pairs={{0,32},{32,64},{64,96},{96,128},{128,160},{160,192},{192,224},{224... | collective-permute-start | bytes 49160 | tf_op jit(solution)/shard_map/ppermute | solution.py:22
  12.0 5.4 %collective-permute-start.3 = (f32[2,4,264]{2,1,0:T(4,128)S(1)}, f32[2,4,264]{2,1,0:T(4,128)S(1)}, u32[]{:S(2)}, u32[]{:S(2)}) collective-permute-start(f32[2,4,264]{2,1,0:T(4,128)S(1)} %get-tuple-element.35), channel_id=1, source_target_pairs={{2,0},{4,2},{6,4},{8,6},{10,8},{12,10},{14,12},{16,14},{18,16},{20... | collective-permute-start | bytes 25352 | tf_op jit(solution)/shard_map/ppermute | solution.py:23
  17.4 13.3 %collective-permute-done.2 = f32[2,4,264]{2,1,0:T(4,128)S(1)} collective-permute-done((f32[2,4,264]{2,1,0:T(4,128)S(1)}, f32[2,4,264]{2,1,0:T(4,128)S(1)}, u32[]{:S(2)}, u32[]{:S(2)}) %collective-permute-start.2) | collective-permute-done | bytes 8480 | tf_op jit(solution)/shard_map/ppermute | solution.py:22
  30.7 2.9 %collective-permute-done.3 = f32[2,4,264]{2,1,0:T(4,128)S(1)} collective-permute-done((f32[2,4,264]{2,1,0:T(4,128)S(1)}, f32[2,4,264]{2,1,0:T(4,128)S(1)}, u32[]{:S(2)}, u32[]{:S(2)}) %collective-permute-start.3) | collective-permute-done | bytes 8480 | tf_op jit(solution)/shard_map/ppermute | solution.py:23
  35.3 5.6 %collective-permute-start.7 = (f32[4,4,2,4,264]{4,3,2,1,0:T(4,128)S(1)}, f32[4,4,2,4,264]{4,3,2,1,0:T(4,128)S(1)}, u32[]{:S(2)}, u32[]{:S(2)}) collective-permute-start(f32[4,4,2,4,264]{4,3,2,1,0:T(4,128)S(1)} %get-tuple-element.13), channel_id=1, source_target_pairs={{2,0},{4,2},{6,4},{8,6},{10,8},{12,10},{14,12},{16,14},{18,16},{20... | collective-permute-start | bytes 405512 | tf_op jit(solution)/shard_map/ppermute | solution.py:23
  41.4 2.8 %collective-permute-done.6 = f32[4,4,2,4,264]{4,3,2,1,0:T(4,128)S(1)} collective-permute-done((f32[4,4,2,4,264]{4,3,2,1,0:T(4,128)S(1)}, f32[4,4,2,4,264]{4,3,2,1,0:T(4,128)S(1)}, u32[]{:S(2)}, u32[]{:S(2)}) %collective-permute-start.6) | collective-permute-done | bytes 135200 | tf_op jit(solution)/shard_map/ppermute | solution.py:22
  47.8 2.1 %broadcast_multiply_fusion.2 = (f32[4,4,2,38,262]{4,3,2,1,0:T(8,128)S(1)}, f32[4,4,2,38,262]{4,3,2,1,0:T(8,128)S(1)}) fusion(f32[38,262]{1,0:T(8,128)S(1)} %slice.362, f32[4,4,2,40,264]{4,3,2,1,0:T(8,128)S(1)} %get-tuple-element.8, f32[4,4,1,38,262]{4,3,2,1,0:T(8,128)S(1)} %get-tuple-element.29, f32[4,4,1,38,262]{4,3,2,1,0:T(8,128)S(1)} %get-tuple-element.28, ...), kind=kLoop, calls=%fused_computation.81 | loop fusion | flops 3185920 | bytes 10274592 | tf_op jit(solution)/shard_map/mul | solution.py:96
  53.4 2.1 %broadcast_multiply_fusion = (f32[4,4,2,34,258]{4,3,2,1,0:T(8,128)S(1)}, f32[4,4,2,34,258]{4,3,2,1,0:T(8,128)S(1)}) fusion(f32[34,258]{1,0:T(8,128)S(1)} %slice.378, f32[4,4,2,36,260]{4,3,2,1,0:T(8,128)S(1)} %get-tuple-element.4, f32[4,4,1,34,258]{4,3,2,1,0:T(8,128)S(1)} %get-tuple-element.25, f32[4,4,1,34,258]{4,3,2,1,0:T(8,128)S(1)} %get-tuple-element.24, ...), kind=kLoop, calls=%fused_computation.77 | loop fusion | flops 2807040 | bytes 9052704 | tf_op jit(solution)/shard_map/mul | solution.py:96
  57.3 2.1 %collective-permute-start.8 = (f32[4,4,2,32,4]{4,3,2,1,0:T(8,128)S(1)}, f32[4,4,2,32,4]{4,3,2,1,0:T(8,128)S(1)}, u32[]{:S(2)}, u32[]{:S(2)}) collective-permute-start(f32[4,4,2,32,4]{4,3,2,1,0:T(8,128)S(1)} %get-tuple-element.30), channel_id=1, source_target_pairs={{0,32},{32,64},{64,96},{96,128},{128,160},{160,192},{192,224},{224... | collective-permute-start | bytes 49160 | tf_op jit(solution)/shard_map/ppermute | solution.py:22
  59.5 12.7 %collective-permute-done.8 = f32[4,4,2,32,4]{4,3,2,1,0:T(8,128)S(1)} collective-permute-done((f32[4,4,2,32,4]{4,3,2,1,0:T(8,128)S(1)}, f32[4,4,2,32,4]{4,3,2,1,0:T(8,128)S(1)}, u32[]{:S(2)}, u32[]{:S(2)}) %collective-permute-start.8) | collective-permute-done | bytes 16416 | tf_op jit(solution)/shard_map/ppermute | solution.py:22
  72.2 11.3 %collective-permute-done.9 = f32[4,4,2,32,4]{4,3,2,1,0:T(8,128)S(1)} collective-permute-done((f32[4,4,2,32,4]{4,3,2,1,0:T(8,128)S(1)}, f32[4,4,2,32,4]{4,3,2,1,0:T(8,128)S(1)}, u32[]{:S(2)}, u32[]{:S(2)}) %collective-permute-start.9) | collective-permute-done | bytes 16416 | tf_op jit(solution)/shard_map/ppermute | solution.py:23
  84.0 5.6 %collective-permute-start.11 = (f32[4,4,2,4,264]{4,3,2,1,0:T(4,128)S(1)}, f32[4,4,2,4,264]{4,3,2,1,0:T(4,128)S(1)}, u32[]{:S(2)}, u32[]{:S(2)}) collective-permute-start(f32[4,4,2,4,264]{4,3,2,1,0:T(4,128)S(1)} %get-tuple-element.11), channel_id=1, source_target_pairs={{2,0},{4,2},{6,4},{8,6},{10,8},{12,10},{14,12},{16,14},{18,16},{20... | collective-permute-start | bytes 405512 | tf_op jit(solution)/shard_map/ppermute | solution.py:23
  89.7 3.7 %collective-permute-done.10 = f32[4,4,2,4,264]{4,3,2,1,0:T(4,128)S(1)} collective-permute-done((f32[4,4,2,4,264]{4,3,2,1,0:T(4,128)S(1)}, f32[4,4,2,4,264]{4,3,2,1,0:T(4,128)S(1)}, u32[]{:S(2)}, u32[]{:S(2)}) %collective-permute-start.10) | collective-permute-done | bytes 135200 | tf_op jit(solution)/shard_map/ppermute | solution.py:22
  95.7 2.2 %fusion.11 = f32[4,4,2,38,262]{4,3,2,1,0:T(8,128)S(1)} fusion(f32[4,4,2,40,264]{4,3,2,1,0:T(8,128)S(1)} %maximum_multiply_fusion.4, f32[4,4,1,38,262]{4,3,2,1,0:T(8,128)S(1)} %get-tuple-element.21, f32[4,4,1,38,262]{4,3,2,1,0:T(8,128)S(1)} %get-tuple-element.20, f32[38,262]{1,0:T(8,128)S(1)} %slice.362, f32[38,262]{1,0:T(8,128)S(1)} %slice.351), kind=kLoop, calls=%fused_computation.21 | loop fusion | flops 3185920 | bytes 9000224 | tf_op jit(solution)/shard_map/mul | solution.py:105
  98.5 2.2 %fusion.7 = f32[4,4,2,36,260]{4,3,2,1,0:T(8,128)S(1)} fusion(f32[4,4,2,38,262]{4,3,2,1,0:T(8,128)S(1)} %fusion.11, f32[4,4,1,36,260]{4,3,2,1,0:T(8,128)S(1)} %get-tuple-element.19, f32[4,4,1,36,260]{4,3,2,1,0:T(8,128)S(1)} %get-tuple-element.18, f32[36,260]{1,0:T(8,128)S(1)} %slice.370, f32[36,260]{1,0:T(8,128)S(1)} %slice.350), kind=kLoop, calls=%fused_computation.13 | loop fusion | flops 2995200 | bytes 8461440 | tf_op jit(solution)/shard_map/mul | solution.py:105
  101.3 2.2 %fusion.3 = f32[4,4,2,34,258]{4,3,2,1,0:T(8,128)S(1)} fusion(f32[4,4,2,36,260]{4,3,2,1,0:T(8,128)S(1)} %fusion.7, f32[4,4,1,34,258]{4,3,2,1,0:T(8,128)S(1)} %get-tuple-element.17, f32[4,4,1,34,258]{4,3,2,1,0:T(8,128)S(1)} %get-tuple-element.16, f32[34,258]{1,0:T(8,128)S(1)} %slice.378, f32[34,258]{1,0:T(8,128)S(1)} %slice.349), kind=kLoop, calls=%fused_computation.5 | loop fusion | flops 2807040 | bytes 7929888 | tf_op jit(solution)/shard_map/mul | solution.py:105
  105.3 10.9 %copy.13 = f32[4,8,8192]{1,0,2:T(4,128)} copy(f32[4,8,8192]{2,1,0:T(8,128)S(1)} %reshape.141) | data formatting | bytes 2097152 | tf_op jit(solution)/shard_map/reshape | solution.py:111
  116.2 21.1 %gather_fusion = f32[2048,4,8]{2,1,0:T(4,128)} fusion(f32[4,8,8192]{1,0,2:T(4,128)} %copy.13, s32[2048]{0:T(1024)S(1)} %broadcast_clamp_fusion), kind=kCustom, calls=%fused_computation | custom fusion | bytes 532480 | tf_op jit(solution)/shard_map/jit(_take)/gather | solution.py:112
  137.3 3.4 %copy.14 = f32[2048,4,8]{0,2,1:T(8,128)S(1)} copy(f32[2048,4,8]{2,1,0:T(4,128)} %gather_fusion) | data formatting | bytes 524288 | tf_op jit(solution)/shard_map/jit(_take)/gather | solution.py:112
  141.9 3.5 %all-to-all-start = ((f32[2,4,16384]{2,1,0:T(4,128)}), f32[2,4,16384]{2,1,0:T(4,128)S(1)}, u32[]{:S(2)}, u32[]{:S(2)}) async-start(f32[2,4,16384]{2,1,0:T(4,128)} %broadcast_in_dim.23), calls=%async_computation | async-start | bytes 1048576 | tf_op jit(solution)/shard_map/all_to_all | solution.py:30
  148.6 10.6 %psum.28 = f32[4,8]{1,0:T(4,128)S(1)} all-reduce(f32[4,8]{1,0:T(4,128)S(1)} %fusion.37), channel_id=1, replica_groups=mesh['lon_0'=4,'lon_1'=2,'lat_0'=8,'lat_1'=2,'rep'=2] {'lon_0'}, use_global_device_ids=true, to_apply=%region_0.1 | all-reduce | flops 32 | bytes 256 | tf_op jit(solution)/shard_map/psum | solution.py:46
  159.2 4.9 %psum.29 = f32[4,8]{1,0:T(4,128)S(1)} all-reduce(f32[4,8]{1,0:T(4,128)S(1)} %psum.28), channel_id=1, replica_groups=mesh['lon_0'=4,'lon_1'=2,'lat_0'=8,'lat_1'=2,'rep'=2] {'lon_1'}, use_global_device_ids=true, to_apply=%region_1.2 | all-reduce | flops 32 | bytes 256 | tf_op jit(solution)/shard_map/psum | solution.py:46
  164.1 18.3 %psum.30 = f32[4,8]{1,0:T(4,128)S(1)} all-reduce(f32[4,8]{1,0:T(4,128)S(1)} %psum.29), channel_id=1, replica_groups=mesh['lon_0'=4,'lon_1'=2,'lat_0'=8,'lat_1'=2,'rep'=2] {'lat_0'}, use_global_device_ids=true, to_apply=%region_2.3 | all-reduce | flops 32 | bytes 256 | tf_op jit(solution)/shard_map/psum | solution.py:46
  182.4 6.4 %psum.31 = f32[4,8]{1,0:T(4,128)S(1)} all-reduce(f32[4,8]{1,0:T(4,128)S(1)} %psum.30), channel_id=1, replica_groups=mesh['lon_0'=4,'lon_1'=2,'lat_0'=8,'lat_1'=2,'rep'=2] {'lat_1'}, use_global_device_ids=true, to_apply=%region_3.4 | all-reduce | flops 32 | bytes 256 | tf_op jit(solution)/shard_map/psum | solution.py:46
  (74 shorter events, 30.3 us)
Async XLA Ops:
  0.6 10.5 %copy-start.2 = (f32[32,256]{1,0:T(8,128)S(1)}, f32[32,256]{1,0:T(8,128)}, u32[]{:S(2)}) copy-start(f32[32,256]{1,0:T(8,128)} %param.8) | copy-start | bytes 98308
  0.6 33.1 %copy-start = (f32[4,4,2,32,256]{4,3,2,1,0:T(8,128)S(1)}, f32[4,4,2,32,256]{4,3,2,1,0:T(8,128)}, u32[]{:S(2)}) copy-start(f32[4,4,2,32,256]{4,3,2,1,0:T(8,128)} %param.7) | copy-start | bytes 3145732
  0.7 9.7 %copy-start.3 = (s32[1,1,2048]{2,1,0:T(1,128)S(1)}, s32[1,1,2048]{2,1,0:T(1,128)}, u32[]{:S(2)}) copy-start(s32[1,1,2048]{2,1,0:T(1,128)} %param.11) | copy-start | bytes 24580
  0.7 10.3 %copy-start.4 = (f32[1,1,2048]{2,1,0:T(1,128)S(1)}, f32[1,1,2048]{2,1,0:T(1,128)}, u32[]{:S(2)}) copy-start(f32[1,1,2048]{2,1,0:T(1,128)} %param.13) | copy-start | bytes 24580
  0.7 10.3 %copy-start.5 = (f32[4]{0:T(128)S(1)}, f32[4]{0:T(128)}, u32[]{:S(2)}) copy-start(f32[4]{0:T(128)} %param.10) | copy-start | bytes 52
  2.3 8.7 %collective-permute-start = (f32[2,32,4]{2,1,0:T(8,128)S(1)}, f32[2,32,4]{2,1,0:T(8,128)S(1)}, u32[]{:S(2)}, u32[]{:S(2)}) collective-permute-start(f32[2,32,4]{2,1,0:T(8,128)S(1)} %get-tuple-element.38), channel_id=1, source_target_pairs={{0,32},{32,64},{64,96},{96,128},{128,160},{160,192},{192,224},{224... | collective-permute-start | bytes 3080 | tf_op jit(solution)/shard_map/ppermute | solution.py:22
  3.9 7.2 %collective-permute-start.1 = (f32[2,32,4]{2,1,0:T(8,128)S(1)}, f32[2,32,4]{2,1,0:T(8,128)S(1)}, u32[]{:S(2)}, u32[]{:S(2)}) collective-permute-start(f32[2,32,4]{2,1,0:T(8,128)S(1)} %get-tuple-element.39), channel_id=1, source_target_pairs={{32,0},{64,32},{96,64},{128,96},{160,128},{192,160},{224,192},{0,2... | collective-permute-start | bytes 3080 | tf_op jit(solution)/shard_map/ppermute | solution.py:23
  6.1 27.6 %collective-permute-start.4 = (f32[4,4,2,32,4]{4,3,2,1,0:T(8,128)S(1)}, f32[4,4,2,32,4]{4,3,2,1,0:T(8,128)S(1)}, u32[]{:S(2)}, u32[]{:S(2)}) collective-permute-start(f32[4,4,2,32,4]{4,3,2,1,0:T(8,128)S(1)} %get-tuple-element.32), channel_id=1, source_target_pairs={{0,32},{32,64},{64,96},{96,128},{128,160},{160,192},{192,224},{224... | collective-permute-start | bytes 49160 | tf_op jit(solution)/shard_map/ppermute | solution.py:22
  8.3 25.4 %collective-permute-start.5 = (f32[4,4,2,32,4]{4,3,2,1,0:T(8,128)S(1)}, f32[4,4,2,32,4]{4,3,2,1,0:T(8,128)S(1)}, u32[]{:S(2)}, u32[]{:S(2)}) collective-permute-start(f32[4,4,2,32,4]{4,3,2,1,0:T(8,128)S(1)} %get-tuple-element.33), channel_id=1, source_target_pairs={{32,0},{64,32},{96,64},{128,96},{160,128},{192,160},{224,192},{0,2... | collective-permute-start | bytes 49160 | tf_op jit(solution)/shard_map/ppermute | solution.py:23
  11.2 19.5 %collective-permute-start.2 = (f32[2,4,264]{2,1,0:T(4,128)S(1)}, f32[2,4,264]{2,1,0:T(4,128)S(1)}, u32[]{:S(2)}, u32[]{:S(2)}) collective-permute-start(f32[2,4,264]{2,1,0:T(4,128)S(1)} %get-tuple-element.34), channel_id=1, source_target_pairs={{0,2},{2,4},{4,6},{6,8},{8,10},{10,12},{12,14},{14,16},{16,18},{18... | collective-permute-start | bytes 25352 | tf_op jit(solution)/shard_map/ppermute | solution.py:22
  12.0 21.6 %collective-permute-start.3 = (f32[2,4,264]{2,1,0:T(4,128)S(1)}, f32[2,4,264]{2,1,0:T(4,128)S(1)}, u32[]{:S(2)}, u32[]{:S(2)}) collective-permute-start(f32[2,4,264]{2,1,0:T(4,128)S(1)} %get-tuple-element.35), channel_id=1, source_target_pairs={{2,0},{4,2},{6,4},{8,6},{10,8},{12,10},{14,12},{16,14},{18,16},{20... | collective-permute-start | bytes 25352 | tf_op jit(solution)/shard_map/ppermute | solution.py:23
  34.1 10.1 %collective-permute-start.6 = (f32[4,4,2,4,264]{4,3,2,1,0:T(4,128)S(1)}, f32[4,4,2,4,264]{4,3,2,1,0:T(4,128)S(1)}, u32[]{:S(2)}, u32[]{:S(2)}) collective-permute-start(f32[4,4,2,4,264]{4,3,2,1,0:T(4,128)S(1)} %get-tuple-element.12), channel_id=1, source_target_pairs={{0,2},{2,4},{4,6},{6,8},{8,10},{10,12},{12,14},{14,16},{16,18},{18... | collective-permute-start | bytes 405512 | tf_op jit(solution)/shard_map/ppermute | solution.py:22
  35.3 10.9 %collective-permute-start.7 = (f32[4,4,2,4,264]{4,3,2,1,0:T(4,128)S(1)}, f32[4,4,2,4,264]{4,3,2,1,0:T(4,128)S(1)}, u32[]{:S(2)}, u32[]{:S(2)}) collective-permute-start(f32[4,4,2,4,264]{4,3,2,1,0:T(4,128)S(1)} %get-tuple-element.13), channel_id=1, source_target_pairs={{2,0},{4,2},{6,4},{8,6},{10,8},{12,10},{14,12},{16,14},{18,16},{20... | collective-permute-start | bytes 405512 | tf_op jit(solution)/shard_map/ppermute | solution.py:23
  57.3 14.9 %collective-permute-start.8 = (f32[4,4,2,32,4]{4,3,2,1,0:T(8,128)S(1)}, f32[4,4,2,32,4]{4,3,2,1,0:T(8,128)S(1)}, u32[]{:S(2)}, u32[]{:S(2)}) collective-permute-start(f32[4,4,2,32,4]{4,3,2,1,0:T(8,128)S(1)} %get-tuple-element.30), channel_id=1, source_target_pairs={{0,32},{32,64},{64,96},{96,128},{128,160},{160,192},{192,224},{224... | collective-permute-start | bytes 49160 | tf_op jit(solution)/shard_map/ppermute | solution.py:22
  59.5 24.0 %collective-permute-start.9 = (f32[4,4,2,32,4]{4,3,2,1,0:T(8,128)S(1)}, f32[4,4,2,32,4]{4,3,2,1,0:T(8,128)S(1)}, u32[]{:S(2)}, u32[]{:S(2)}) collective-permute-start(f32[4,4,2,32,4]{4,3,2,1,0:T(8,128)S(1)} %get-tuple-element.31), channel_id=1, source_target_pairs={{32,0},{64,32},{96,64},{128,96},{160,128},{192,160},{224,192},{0,2... | collective-permute-start | bytes 49160 | tf_op jit(solution)/shard_map/ppermute | solution.py:23
  83.9 9.5 %collective-permute-start.10 = (f32[4,4,2,4,264]{4,3,2,1,0:T(4,128)S(1)}, f32[4,4,2,4,264]{4,3,2,1,0:T(4,128)S(1)}, u32[]{:S(2)}, u32[]{:S(2)}) collective-permute-start(f32[4,4,2,4,264]{4,3,2,1,0:T(4,128)S(1)} %get-tuple-element.10), channel_id=1, source_target_pairs={{0,2},{2,4},{4,6},{6,8},{8,10},{10,12},{12,14},{14,16},{16,18},{18... | collective-permute-start | bytes 405512 | tf_op jit(solution)/shard_map/ppermute | solution.py:22
  84.0 10.2 %collective-permute-start.11 = (f32[4,4,2,4,264]{4,3,2,1,0:T(4,128)S(1)}, f32[4,4,2,4,264]{4,3,2,1,0:T(4,128)S(1)}, u32[]{:S(2)}, u32[]{:S(2)}) collective-permute-start(f32[4,4,2,4,264]{4,3,2,1,0:T(4,128)S(1)} %get-tuple-element.11), channel_id=1, source_target_pairs={{2,0},{4,2},{6,4},{8,6},{10,8},{12,10},{14,12},{16,14},{18,16},{20... | collective-permute-start | bytes 405512 | tf_op jit(solution)/shard_map/ppermute | solution.py:23
  105.1 11.1 %copy-start.1 = (f32[4,4,2,32,256]{4,3,2,1,0:T(8,128)}, f32[4,4,2,32,256]{4,3,2,1,0:T(8,128)S(1)}, u32[]{:S(2)}) copy-start(f32[4,4,2,32,256]{4,3,2,1,0:T(8,128)S(1)} %fusion.24) | copy-start | bytes 3145732
  141.9 5.2 %all-to-all-start = ((f32[2,4,16384]{2,1,0:T(4,128)}), f32[2,4,16384]{2,1,0:T(4,128)S(1)}, u32[]{:S(2)}, u32[]{:S(2)}) async-start(f32[2,4,16384]{2,1,0:T(4,128)} %broadcast_in_dim.23), calls=%async_computation | async-start | bytes 1048576 | tf_op jit(solution)/shard_map/all_to_all | solution.py:30
where the time goes:
time: 190 us; the launch traced here: 189 us
  waiting for transfers between devices  51 us (27%)
  blocking collectives  40.3 us (21%)
  local copies, waits for them, and re-layouts  39.4 us (21%)
  starting transfers between devices  30.8 us (16%)
  other arithmetic  25 us (13%)
    psum x4, blocking collectives, one_axis_at_a_time(): shard = lax.psum(shard, axis)  40.3 us
    ppermute x6, waiting for transfers between devices, padded_2(): before = lax.ppermute(last, axis, up)  32.4 us
    gather x2, local copies, waits for them, and re-layouts, local(): samples = jnp.take(flat, site_cell[0, 0], axis=2)  24.5 us
    ppermute x6, starting transfers between devices, padded_2(): after = lax.ppermute(leading, axis, down)  19.3 us
    ppermute x6, waiting for transfers between devices, padded_2(): after = lax.ppermute(leading, axis, down)  17 us
    reshape x2, local copies, waits for them, and re-layouts, local(): flat = current.reshape(rep_local, CONST * 2, rows_lat * cols_lon)  11.1 us
    mul x5, other arithmetic, local(): window(wet_ext, width - 1)  8.83 us
    ppermute x6, starting transfers between devices, padded_2(): before = lax.ppermute(last, axis, up)  7.99 us
  transfers between devices with their start and end apart: 13, of which 9 were waited for; matrix products, arithmetic and copies ran while one was open for 1% of the time, Pallas kernels for 0%

commit v1 on v0

--- a/solution.py
+++ b/solution.py
@@ -43,7 +43,8 @@
 
 def one_axis_at_a_time(shard, axes):
     for axis in axes:
-        shard = lax.psum(shard, axis)
+        shards = lax.all_gather(shard, axis)
+        shard = jnp.sum(shards, axis=0)
     return shard
 
 

time: 190 us -> 197 us (1.037)
  blocking collectives: 40.3 us -> 47.3 us
    all_gather x0 -> x4, blocking collectives: none -> 47.3 us  [one_axis_at_a_time(): shards = lax.all_gather(shard, axis)]
    psum x4 -> x0, blocking collectives: 40.3 us -> none  [one_axis_at_a_time(): shard = lax.psum(shard, axis)]
where the time goes in v1:
time: 197 us
  waiting for transfers between devices  51 us (26%)
  blocking collectives  47.3 us (24%)
  local copies, waits for them, and re-layouts  39.4 us (20%)
  starting transfers between devices  30.8 us (16%)
  other arithmetic  25.1 us (13%)
    all_gather x4, blocking collectives, one_axis_at_a_time(): shards = lax.all_gather(shard, axis)  47.3 us
    ppermute x6, waiting for transfers between devices, padded_2(): before = lax.ppermute(last, axis, up)  32.4 us
    gather x2, local copies, waits for them, and re-layouts, local(): samples = jnp.take(flat, site_cell[0, 0], axis=2)  24.5 us
    ppermute x6, starting transfers between devices, padded_2(): after = lax.ppermute(leading, axis, down)  19.3 us
    ppermute x6, waiting for transfers between devices, padded_2(): after = lax.ppermute(leading, axis, down)  17 us
    reshape x2, local copies, waits for them, and re-layouts, local(): flat = current.reshape(rep_local, CONST * 2, rows_lat * cols_lon)  11.1 us
    mul x5, other arithmetic, local(): window(wet_ext, width - 1)  8.83 us
    ppermute x6, starting transfers between devices, padded_2(): before = lax.ppermute(last, axis, up)  7.99 us
  transfers between devices with their start and end apart: 13, of which 9 were waited for; matrix products, arithmetic and copies ran while one was open for 1% of the time, Pallas kernels for 0%

profile of v1, /device:TPU:2, one launch (start us, length us, event | category | flops | bytes accessed | tf_op | source)
XLA Modules:
  0.0 196.5 jit_solution(9666463336009877773)
XLA Ops:
  6.1 2.2 %collective-permute-start.4 = (f32[4,4,2,32,4]{4,3,2,1,0:T(8,128)S(1)}, f32[4,4,2,32,4]{4,3,2,1,0:T(8,128)S(1)}, u32[]{:S(2)}, u32[]{:S(2)}) collective-permute-start(f32[4,4,2,32,4]{4,3,2,1,0:T(8,128)S(1)} %get-tuple-element.32), channel_id=1, source_target_pairs={{0,32},{32,64},{64,96},{96,128},{128,160},{160,192},{192,224},{224... | collective-permute-start | bytes 49160 | tf_op jit(solution)/shard_map/ppermute | solution.py:22
  12.0 5.4 %collective-permute-start.3 = (f32[2,4,264]{2,1,0:T(4,128)S(1)}, f32[2,4,264]{2,1,0:T(4,128)S(1)}, u32[]{:S(2)}, u32[]{:S(2)}) collective-permute-start(f32[2,4,264]{2,1,0:T(4,128)S(1)} %get-tuple-element.35), channel_id=1, source_target_pairs={{2,0},{4,2},{6,4},{8,6},{10,8},{12,10},{14,12},{16,14},{18,16},{20... | collective-permute-start | bytes 25352 | tf_op jit(solution)/shard_map/ppermute | solution.py:23
  17.4 13.3 %collective-permute-done.2 = f32[2,4,264]{2,1,0:T(4,128)S(1)} collective-permute-done((f32[2,4,264]{2,1,0:T(4,128)S(1)}, f32[2,4,264]{2,1,0:T(4,128)S(1)}, u32[]{:S(2)}, u32[]{:S(2)}) %collective-permute-start.2) | collective-permute-done | bytes 8480 | tf_op jit(solution)/shard_map/ppermute | solution.py:22
  30.7 2.9 %collective-permute-done.3 = f32[2,4,264]{2,1,0:T(4,128)S(1)} collective-permute-done((f32[2,4,264]{2,1,0:T(4,128)S(1)}, f32[2,4,264]{2,1,0:T(4,128)S(1)}, u32[]{:S(2)}, u32[]{:S(2)}) %collective-permute-start.3) | collective-permute-done | bytes 8480 | tf_op jit(solution)/shard_map/ppermute | solution.py:23
  35.3 5.6 %collective-permute-start.7 = (f32[4,4,2,4,264]{4,3,2,1,0:T(4,128)S(1)}, f32[4,4,2,4,264]{4,3,2,1,0:T(4,128)S(1)}, u32[]{:S(2)}, u32[]{:S(2)}) collective-permute-start(f32[4,4,2,4,264]{4,3,2,1,0:T(4,128)S(1)} %get-tuple-element.13), channel_id=1, source_target_pairs={{2,0},{4,2},{6,4},{8,6},{10,8},{12,10},{14,12},{16,14},{18,16},{20... | collective-permute-start | bytes 405512 | tf_op jit(solution)/shard_map/ppermute | solution.py:23
  41.4 2.8 %collective-permute-done.6 = f32[4,4,2,4,264]{4,3,2,1,0:T(4,128)S(1)} collective-permute-done((f32[4,4,2,4,264]{4,3,2,1,0:T(4,128)S(1)}, f32[4,4,2,4,264]{4,3,2,1,0:T(4,128)S(1)}, u32[]{:S(2)}, u32[]{:S(2)}) %collective-permute-start.6) | collective-permute-done | bytes 135200 | tf_op jit(solution)/shard_map/ppermute | solution.py:22
  47.8 2.1 %broadcast_multiply_fusion.2 = (f32[4,4,2,38,262]{4,3,2,1,0:T(8,128)S(1)}, f32[4,4,2,38,262]{4,3,2,1,0:T(8,128)S(1)}) fusion(f32[38,262]{1,0:T(8,128)S(1)} %slice.362, f32[4,4,2,40,264]{4,3,2,1,0:T(8,128)S(1)} %get-tuple-element.8, f32[4,4,1,38,262]{4,3,2,1,0:T(8,128)S(1)} %get-tuple-element.29, f32[4,4,1,38,262]{4,3,2,1,0:T(8,128)S(1)} %get-tuple-element.28, ...), kind=kLoop, calls=%fused_computation.82 | loop fusion | flops 3185920 | bytes 10274592 | tf_op jit(solution)/shard_map/mul | solution.py:97
  53.4 2.1 %broadcast_multiply_fusion = (f32[4,4,2,34,258]{4,3,2,1,0:T(8,128)S(1)}, f32[4,4,2,34,258]{4,3,2,1,0:T(8,128)S(1)}) fusion(f32[34,258]{1,0:T(8,128)S(1)} %slice.378, f32[4,4,2,36,260]{4,3,2,1,0:T(8,128)S(1)} %get-tuple-element.4, f32[4,4,1,34,258]{4,3,2,1,0:T(8,128)S(1)} %get-tuple-element.25, f32[4,4,1,34,258]{4,3,2,1,0:T(8,128)S(1)} %get-tuple-element.24, ...), kind=kLoop, calls=%fused_computation.78 | loop fusion | flops 2807040 | bytes 9052704 | tf_op jit(solution)/shard_map/mul | solution.py:97
  57.3 2.1 %collective-permute-start.8 = (f32[4,4,2,32,4]{4,3,2,1,0:T(8,128)S(1)}, f32[4,4,2,32,4]{4,3,2,1,0:T(8,128)S(1)}, u32[]{:S(2)}, u32[]{:S(2)}) collective-permute-start(f32[4,4,2,32,4]{4,3,2,1,0:T(8,128)S(1)} %get-tuple-element.30), channel_id=1, source_target_pairs={{0,32},{32,64},{64,96},{96,128},{128,160},{160,192},{192,224},{224... | collective-permute-start | bytes 49160 | tf_op jit(solution)/shard_map/ppermute | solution.py:22
  59.5 12.7 %collective-permute-done.8 = f32[4,4,2,32,4]{4,3,2,1,0:T(8,128)S(1)} collective-permute-done((f32[4,4,2,32,4]{4,3,2,1,0:T(8,128)S(1)}, f32[4,4,2,32,4]{4,3,2,1,0:T(8,128)S(1)}, u32[]{:S(2)}, u32[]{:S(2)}) %collective-permute-start.8) | collective-permute-done | bytes 16416 | tf_op jit(solution)/shard_map/ppermute | solution.py:22
  72.2 11.3 %collective-permute-done.9 = f32[4,4,2,32,4]{4,3,2,1,0:T(8,128)S(1)} collective-permute-done((f32[4,4,2,32,4]{4,3,2,1,0:T(8,128)S(1)}, f32[4,4,2,32,4]{4,3,2,1,0:T(8,128)S(1)}, u32[]{:S(2)}, u32[]{:S(2)}) %collective-permute-start.9) | collective-permute-done | bytes 16416 | tf_op jit(solution)/shard_map/ppermute | solution.py:23
  84.0 5.6 %collective-permute-start.11 = (f32[4,4,2,4,264]{4,3,2,1,0:T(4,128)S(1)}, f32[4,4,2,4,264]{4,3,2,1,0:T(4,128)S(1)}, u32[]{:S(2)}, u32[]{:S(2)}) collective-permute-start(f32[4,4,2,4,264]{4,3,2,1,0:T(4,128)S(1)} %get-tuple-element.11), channel_id=1, source_target_pairs={{2,0},{4,2},{6,4},{8,6},{10,8},{12,10},{14,12},{16,14},{18,16},{20... | collective-permute-start | bytes 405512 | tf_op jit(solution)/shard_map/ppermute | solution.py:23
  89.7 3.7 %collective-permute-done.10 = f32[4,4,2,4,264]{4,3,2,1,0:T(4,128)S(1)} collective-permute-done((f32[4,4,2,4,264]{4,3,2,1,0:T(4,128)S(1)}, f32[4,4,2,4,264]{4,3,2,1,0:T(4,128)S(1)}, u32[]{:S(2)}, u32[]{:S(2)}) %collective-permute-start.10) | collective-permute-done | bytes 135200 | tf_op jit(solution)/shard_map/ppermute | solution.py:22
  95.7 2.2 %fusion.11 = f32[4,4,2,38,262]{4,3,2,1,0:T(8,128)S(1)} fusion(f32[4,4,2,40,264]{4,3,2,1,0:T(8,128)S(1)} %maximum_multiply_fusion.4, f32[4,4,1,38,262]{4,3,2,1,0:T(8,128)S(1)} %get-tuple-element.21, f32[4,4,1,38,262]{4,3,2,1,0:T(8,128)S(1)} %get-tuple-element.20, f32[38,262]{1,0:T(8,128)S(1)} %slice.362, f32[38,262]{1,0:T(8,128)S(1)} %slice.351), kind=kLoop, calls=%fused_computation.21 | loop fusion | flops 3185920 | bytes 9000224 | tf_op jit(solution)/shard_map/mul | solution.py:106
  98.5 2.2 %fusion.7 = f32[4,4,2,36,260]{4,3,2,1,0:T(8,128)S(1)} fusion(f32[4,4,2,38,262]{4,3,2,1,0:T(8,128)S(1)} %fusion.11, f32[4,4,1,36,260]{4,3,2,1,0:T(8,128)S(1)} %get-tuple-element.19, f32[4,4,1,36,260]{4,3,2,1,0:T(8,128)S(1)} %get-tuple-element.18, f32[36,260]{1,0:T(8,128)S(1)} %slice.370, f32[36,260]{1,0:T(8,128)S(1)} %slice.350), kind=kLoop, calls=%fused_computation.13 | loop fusion | flops 2995200 | bytes 8461440 | tf_op jit(solution)/shard_map/mul | solution.py:106
  101.3 2.2 %fusion.3 = f32[4,4,2,34,258]{4,3,2,1,0:T(8,128)S(1)} fusion(f32[4,4,2,36,260]{4,3,2,1,0:T(8,128)S(1)} %fusion.7, f32[4,4,1,34,258]{4,3,2,1,0:T(8,128)S(1)} %get-tuple-element.17, f32[4,4,1,34,258]{4,3,2,1,0:T(8,128)S(1)} %get-tuple-element.16, f32[34,258]{1,0:T(8,128)S(1)} %slice.378, f32[34,258]{1,0:T(8,128)S(1)} %slice.349), kind=kLoop, calls=%fused_computation.5 | loop fusion | flops 2807040 | bytes 7929888 | tf_op jit(solution)/shard_map/mul | solution.py:106
  105.3 10.9 %copy.16 = f32[4,8,8192]{1,0,2:T(4,128)} copy(f32[4,8,8192]{2,1,0:T(8,128)S(1)} %reshape.141) | data formatting | bytes 2097152 | tf_op jit(solution)/shard_map/reshape | solution.py:112
  116.2 21.1 %gather_fusion = f32[2048,4,8]{2,1,0:T(4,128)} fusion(f32[4,8,8192]{1,0,2:T(4,128)} %copy.16, s32[2048]{0:T(1024)S(1)} %broadcast_clamp_fusion), kind=kCustom, calls=%fused_computation | custom fusion | bytes 532480 | tf_op jit(solution)/shard_map/jit(_take)/gather | solution.py:113
  137.3 3.4 %copy.17 = f32[2048,4,8]{0,2,1:T(8,128)S(1)} copy(f32[2048,4,8]{2,1,0:T(4,128)} %gather_fusion) | data formatting | bytes 524288 | tf_op jit(solution)/shard_map/jit(_take)/gather | solution.py:113
  141.9 3.5 %all-to-all-start = ((f32[2,4,16384]{2,1,0:T(4,128)}), f32[2,4,16384]{2,1,0:T(4,128)S(1)}, u32[]{:S(2)}, u32[]{:S(2)}) async-start(f32[2,4,16384]{2,1,0:T(4,128)} %broadcast_in_dim.23), calls=%async_computation | async-start | bytes 1048576 | tf_op jit(solution)/shard_map/all_to_all | solution.py:30
  148.6 10.4 %all-gather.4 = f32[4,4,8]{2,1,0:T(4,128)S(1)} all-gather(f32[1,4,8]{2,1,0:T(4,128)S(1)} %convolution_bitcast_fusion), channel_id=2, replica_groups=mesh['lon_0'=4,'lon_1'=2,'lat_0'=8,'lat_1'=2,'rep'=2] {'lon_0'}, dimensions={0}, use_global_device_ids=true | all-gather | bytes 640 | tf_op jit(solution)/shard_map/all_gather | solution.py:46
  159.0 4.4 %all-gather.5 = f32[2,4,8]{2,1,0:T(4,128)S(1)} all-gather(f32[1,4,8]{2,1,0:T(4,128)S(1)} %bitcast.49), channel_id=3, replica_groups=mesh['lon_0'=4,'lon_1'=2,'lat_0'=8,'lat_1'=2,'rep'=2] {'lon_1'}, dimensions={0}, use_global_device_ids=true | all-gather | bytes 384 | tf_op jit(solution)/shard_map/all_gather | solution.py:46
  163.4 26.6 %all-gather.6 = f32[8,4,8]{2,1,0:T(4,128)S(1)} all-gather(f32[1,4,8]{2,1,0:T(4,128)S(1)} %bitcast.48), channel_id=4, replica_groups=mesh['lon_0'=4,'lon_1'=2,'lat_0'=8,'lat_1'=2,'rep'=2] {'lat_0'}, dimensions={0}, use_global_device_ids=true | all-gather | bytes 1152 | tf_op jit(solution)/shard_map/all_gather | solution.py:46
  190.1 5.9 %all-gather.7 = f32[2,4,8]{2,1,0:T(4,128)S(1)} all-gather(f32[1,4,8]{2,1,0:T(4,128)S(1)} %bitcast.47), channel_id=5, replica_groups=mesh['lon_0'=4,'lon_1'=2,'lat_0'=8,'lat_1'=2,'rep'=2] {'lat_1'}, dimensions={0}, use_global_device_ids=true | all-gather | bytes 384 | tf_op jit(solution)/shard_map/all_gather | solution.py:46
  (78 shorter events, 30.4 us)
Async XLA Ops:
  0.6 10.5 %copy-start.2 = (f32[32,256]{1,0:T(8,128)S(1)}, f32[32,256]{1,0:T(8,128)}, u32[]{:S(2)}) copy-start(f32[32,256]{1,0:T(8,128)} %param.8) | copy-start | bytes 98308
  0.6 33.1 %copy-start = (f32[4,4,2,32,256]{4,3,2,1,0:T(8,128)S(1)}, f32[4,4,2,32,256]{4,3,2,1,0:T(8,128)}, u32[]{:S(2)}) copy-start(f32[4,4,2,32,256]{4,3,2,1,0:T(8,128)} %param.7) | copy-start | bytes 3145732
  0.7 9.7 %copy-start.3 = (s32[1,1,2048]{2,1,0:T(1,128)S(1)}, s32[1,1,2048]{2,1,0:T(1,128)}, u32[]{:S(2)}) copy-start(s32[1,1,2048]{2,1,0:T(1,128)} %param.11) | copy-start | bytes 24580
  0.7 10.3 %copy-start.4 = (f32[1,1,2048]{2,1,0:T(1,128)S(1)}, f32[1,1,2048]{2,1,0:T(1,128)}, u32[]{:S(2)}) copy-start(f32[1,1,2048]{2,1,0:T(1,128)} %param.13) | copy-start | bytes 24580
  0.7 10.3 %copy-start.5 = (f32[4]{0:T(128)S(1)}, f32[4]{0:T(128)}, u32[]{:S(2)}) copy-start(f32[4]{0:T(128)} %param.10) | copy-start | bytes 52
  2.3 8.7 %collective-permute-start = (f32[2,32,4]{2,1,0:T(8,128)S(1)}, f32[2,32,4]{2,1,0:T(8,128)S(1)}, u32[]{:S(2)}, u32[]{:S(2)}) collective-permute-start(f32[2,32,4]{2,1,0:T(8,128)S(1)} %get-tuple-element.38), channel_id=1, source_target_pairs={{0,32},{32,64},{64,96},{96,128},{128,160},{160,192},{192,224},{224... | collective-permute-start | bytes 3080 | tf_op jit(solution)/shard_map/ppermute | solution.py:22
  3.9 7.2 %collective-permute-start.1 = (f32[2,32,4]{2,1,0:T(8,128)S(1)}, f32[2,32,4]{2,1,0:T(8,128)S(1)}, u32[]{:S(2)}, u32[]{:S(2)}) collective-permute-start(f32[2,32,4]{2,1,0:T(8,128)S(1)} %get-tuple-element.39), channel_id=1, source_target_pairs={{32,0},{64,32},{96,64},{128,96},{160,128},{192,160},{224,192},{0,2... | collective-permute-start | bytes 3080 | tf_op jit(solution)/shard_map/ppermute | solution.py:23
  6.1 27.6 %collective-permute-start.4 = (f32[4,4,2,32,4]{4,3,2,1,0:T(8,128)S(1)}, f32[4,4,2,32,4]{4,3,2,1,0:T(8,128)S(1)}, u32[]{:S(2)}, u32[]{:S(2)}) collective-permute-start(f32[4,4,2,32,4]{4,3,2,1,0:T(8,128)S(1)} %get-tuple-element.32), channel_id=1, source_target_pairs={{0,32},{32,64},{64,96},{96,128},{128,160},{160,192},{192,224},{224... | collective-permute-start | bytes 49160 | tf_op jit(solution)/shard_map/ppermute | solution.py:22
  8.3 25.4 %collective-permute-start.5 = (f32[4,4,2,32,4]{4,3,2,1,0:T(8,128)S(1)}, f32[4,4,2,32,4]{4,3,2,1,0:T(8,128)S(1)}, u32[]{:S(2)}, u32[]{:S(2)}) collective-permute-start(f32[4,4,2,32,4]{4,3,2,1,0:T(8,128)S(1)} %get-tuple-element.33), channel_id=1, source_target_pairs={{32,0},{64,32},{96,64},{128,96},{160,128},{192,160},{224,192},{0,2... | collective-permute-start | bytes 49160 | tf_op jit(solution)/shard_map/ppermute | solution.py:23
  11.2 19.5 %collective-permute-start.2 = (f32[2,4,264]{2,1,0:T(4,128)S(1)}, f32[2,4,264]{2,1,0:T(4,128)S(1)}, u32[]{:S(2)}, u32[]{:S(2)}) collective-permute-start(f32[2,4,264]{2,1,0:T(4,128)S(1)} %get-tuple-element.34), channel_id=1, source_target_pairs={{0,2},{2,4},{4,6},{6,8},{8,10},{10,12},{12,14},{14,16},{16,18},{18... | collective-permute-start | bytes 25352 | tf_op jit(solution)/shard_map/ppermute | solution.py:22
  12.0 21.6 %collective-permute-start.3 = (f32[2,4,264]{2,1,0:T(4,128)S(1)}, f32[2,4,264]{2,1,0:T(4,128)S(1)}, u32[]{:S(2)}, u32[]{:S(2)}) collective-permute-start(f32[2,4,264]{2,1,0:T(4,128)S(1)} %get-tuple-element.35), channel_id=1, source_target_pairs={{2,0},{4,2},{6,4},{8,6},{10,8},{12,10},{14,12},{16,14},{18,16},{20... | collective-permute-start | bytes 25352 | tf_op jit(solution)/shard_map/ppermute | solution.py:23
  34.1 10.1 %collective-permute-start.6 = (f32[4,4,2,4,264]{4,3,2,1,0:T(4,128)S(1)}, f32[4,4,2,4,264]{4,3,2,1,0:T(4,128)S(1)}, u32[]{:S(2)}, u32[]{:S(2)}) collective-permute-start(f32[4,4,2,4,264]{4,3,2,1,0:T(4,128)S(1)} %get-tuple-element.12), channel_id=1, source_target_pairs={{0,2},{2,4},{4,6},{6,8},{8,10},{10,12},{12,14},{14,16},{16,18},{18... | collective-permute-start | bytes 405512 | tf_op jit(solution)/shard_map/ppermute | solution.py:22
  35.3 10.9 %collective-permute-start.7 = (f32[4,4,2,4,264]{4,3,2,1,0:T(4,128)S(1)}, f32[4,4,2,4,264]{4,3,2,1,0:T(4,128)S(1)}, u32[]{:S(2)}, u32[]{:S(2)}) collective-permute-start(f32[4,4,2,4,264]{4,3,2,1,0:T(4,128)S(1)} %get-tuple-element.13), channel_id=1, source_target_pairs={{2,0},{4,2},{6,4},{8,6},{10,8},{12,10},{14,12},{16,14},{18,16},{20... | collective-permute-start | bytes 405512 | tf_op jit(solution)/shard_map/ppermute | solution.py:23
  57.3 14.9 %collective-permute-start.8 = (f32[4,4,2,32,4]{4,3,2,1,0:T(8,128)S(1)}, f32[4,4,2,32,4]{4,3,2,1,0:T(8,128)S(1)}, u32[]{:S(2)}, u32[]{:S(2)}) collective-permute-start(f32[4,4,2,32,4]{4,3,2,1,0:T(8,128)S(1)} %get-tuple-element.30), channel_id=1, source_target_pairs={{0,32},{32,64},{64,96},{96,128},{128,160},{160,192},{192,224},{224... | collective-permute-start | bytes 49160 | tf_op jit(solution)/shard_map/ppermute | solution.py:22
  59.5 24.0 %collective-permute-start.9 = (f32[4,4,2,32,4]{4,3,2,1,0:T(8,128)S(1)}, f32[4,4,2,32,4]{4,3,2,1,0:T(8,128)S(1)}, u32[]{:S(2)}, u32[]{:S(2)}) collective-permute-start(f32[4,4,2,32,4]{4,3,2,1,0:T(8,128)S(1)} %get-tuple-element.31), channel_id=1, source_target_pairs={{32,0},{64,32},{96,64},{128,96},{160,128},{192,160},{224,192},{0,2... | collective-permute-start | bytes 49160 | tf_op jit(solution)/shard_map/ppermute | solution.py:23
  83.9 9.5 %collective-permute-start.10 = (f32[4,4,2,4,264]{4,3,2,1,0:T(4,128)S(1)}, f32[4,4,2,4,264]{4,3,2,1,0:T(4,128)S(1)}, u32[]{:S(2)}, u32[]{:S(2)}) collective-permute-start(f32[4,4,2,4,264]{4,3,2,1,0:T(4,128)S(1)} %get-tuple-element.10), channel_id=1, source_target_pairs={{0,2},{2,4},{4,6},{6,8},{8,10},{10,12},{12,14},{14,16},{16,18},{18... | collective-permute-start | bytes 405512 | tf_op jit(solution)/shard_map/ppermute | solution.py:22
  84.0 10.2 %collective-permute-start.11 = (f32[4,4,2,4,264]{4,3,2,1,0:T(4,128)S(1)}, f32[4,4,2,4,264]{4,3,2,1,0:T(4,128)S(1)}, u32[]{:S(2)}, u32[]{:S(2)}) collective-permute-start(f32[4,4,2,4,264]{4,3,2,1,0:T(4,128)S(1)} %get-tuple-element.11), channel_id=1, source_target_pairs={{2,0},{4,2},{6,4},{8,6},{10,8},{12,10},{14,12},{16,14},{18,16},{20... | collective-permute-start | bytes 405512 | tf_op jit(solution)/shard_map/ppermute | solution.py:23
  105.1 11.1 %copy-start.1 = (f32[4,4,2,32,256]{4,3,2,1,0:T(8,128)}, f32[4,4,2,32,256]{4,3,2,1,0:T(8,128)S(1)}, u32[]{:S(2)}) copy-start(f32[4,4,2,32,256]{4,3,2,1,0:T(8,128)S(1)} %fusion.24) | copy-start | bytes 3145732
  141.9 5.2 %all-to-all-start = ((f32[2,4,16384]{2,1,0:T(4,128)}), f32[2,4,16384]{2,1,0:T(4,128)S(1)}, u32[]{:S(2)}, u32[]{:S(2)}) async-start(f32[2,4,16384]{2,1,0:T(4,128)} %broadcast_in_dim.23), calls=%async_computation | async-start | bytes 1048576 | tf_op jit(solution)/shard_map/all_to_all | solution.py:30
